TPU v7x, 32 devices: a whole 2x2x4 slice. The times are simulated.
32 devices in a mesh: groups: 2 (over y), samples: 8 (over z, x), section: 1, mp: 2 (over core).
Axes of the slice: x: 2, y: 2, z: 4, core: 2. Of those that a mesh axis runs over, the one named last changes fastest.
Arguments:
- stored_inputs: bfloat16 [1, 16, 128, 2048], P('section', ('groups', 'samples'), None, 'mp'), parts along dimension 1
- top_cotangent: bfloat16 [16, 128, 2048], P(('groups', 'samples'), None, 'mp'), parts along dimension 0, may hold values from -0.375 to 0.375
- layer_weights: bfloat16 [1, 2048, 2048], P('section', 'samples', 'mp'), may hold values from -0.125 to 0.125
- block_layout: int32 [1, 2, 2], P('section'), may hold values 0 or 1
- region_mask: int32 [128], replicated, may hold values from 0 to 1, as said below
- partner_samples: int32 [16], P('groups'), parts along dimension 0, may hold values from 0 to 7, as said below
- spins: int32 [16, 128], P(('groups', 'samples')), parts along dimension 0, may hold values from 0 to 1
Outputs:
- weight_grad: float32 [2, 2048, 2048], P(('groups', 'section'), 'samples', 'mp'), parts along dimension 0
- layer_cotangents: bfloat16 [1, 16, 128, 2048], P('section', ('groups', 'samples'), None, 'mp'), parts along dimension 1
- embed_grad: float32 [4, 2048], P('groups', 'mp'), parts along dimension 0
There are 2 independent parts, one for each index of `groups`. A program takes and returns all parts, laid end to end along the dimension named above; an argument that names none is the same for every part. Nothing has to cross between parts.
Inputs may be any that keep to these rules, and one draw needn't show every extreme that they name: `region_mask`: exactly 64 of the 128 entries are 1, the others 0. The samples pair up: partner_samples[partner_samples[r]] = r and partner_samples[r] != r for every sample r. `block_layout`: a query block always sees its own block, whatever the diagonal entry holds.
All inputs are finite; a program needn't handle non-finite values.
Results may differ from a plain program's by a relative error of at most 0.03.
Values may be sent and summed in bfloat16 or wider, within the bound.
A program may use at most 64 MiB of HBM per device.

v0:
```python
import jax
import jax.numpy as jnp
from jax import lax
from jax.sharding import PartitionSpec as P

HEAD = 128
BLOCK = 64
SPINS = 2


def for_sending(value):

    def short(part):
        return part.astype(jnp.bfloat16) if part.dtype == jnp.float32 else part

    return jax.tree.map(short, value)


def passed_along(block, axis, distance):
    devices = range(lax.axis_size(axis))
    route = [(i - distance, i) for i in devices if i - distance in devices]
    return lax.ppermute(block, axis, route)


def softmax_parts(inputs_h, allowed, attention_scale):
    scores = (
        jnp.einsum("qhd,khd->hqk", inputs_h, inputs_h, preferred_element_type=jnp.float32)
        * attention_scale
    )
    scores = jnp.where(allowed[None], scores, -jnp.inf)
    top_score = jnp.max(scores, axis=-1, keepdims=True)
    expo_terms = jnp.exp(scores - top_score)
    probs = expo_terms / jnp.sum(expo_terms, axis=-1, keepdims=True)
    return (probs, probs.astype(jnp.bfloat16))


def local(
    stored_inputs, top_cotangent, layer_weights, block_layout, region_mask, partner_samples, spins
):
    section_index = lax.axis_index("section")
    section_count = lax.axis_size("section")
    micro_count = stored_inputs.shape[1]
    seq_len = stored_inputs.shape[2]
    half_width = stored_inputs.shape[3]
    head_count = half_width // HEAD
    attention_scale = 4.0 / HEAD
    weights = lax.all_gather(layer_weights[0], "samples", axis=0, tiled=True)
    pos_block = jnp.arange(seq_len) // BLOCK
    block_onehot = (pos_block[:, None] == jnp.arange(block_layout.shape[1])[None, :]).astype(
        jnp.float32
    )
    linked = jnp.dot(jnp.dot(block_onehot, block_layout[0].astype(jnp.float32)), block_onehot.T)
    allowed = (linked > 0.5) | (pos_block[:, None] == pos_block[None, :])
    every_layer_input = stored_inputs[0]
    inputs_h = every_layer_input[0].reshape(seq_len, head_count, HEAD)
    probs, probs_low = softmax_parts(inputs_h, allowed, attention_scale)
    attended = jnp.einsum(
        "hqk,khd->qhd", probs_low, inputs_h, preferred_element_type=jnp.float32
    ).astype(jnp.bfloat16)
    probs_list = [probs]
    low_list = [probs_low]
    attend_list = [attended.reshape(seq_len, half_width)]
    probs_all = jnp.stack(probs_list)
    low_all = jnp.stack(low_list)
    attend_store = jnp.stack(attend_list)

    def layer_back(grad_full, grad_own, inputs, probs, probs_low):
        grad_attn = jnp.dot(grad_full, weights, preferred_element_type=jnp.float32).astype(
            jnp.bfloat16
        )
        inputs_h = inputs.reshape(seq_len, head_count, HEAD)
        grad_h = grad_attn.reshape(seq_len, head_count, HEAD)
        grad_probs = jnp.einsum(
            "qhd,khd->hqk", grad_h, inputs_h, preferred_element_type=jnp.float32
        )
        grad_scores = (
            probs * (grad_probs - jnp.sum(grad_probs * probs, axis=-1, keepdims=True))
        ).astype(jnp.bfloat16)
        through = jnp.einsum("hqk,qhd->khd", probs_low, grad_h, preferred_element_type=jnp.float32)
        through = through + attention_scale * (
            jnp.einsum("hqk,khd->qhd", grad_scores, inputs_h, preferred_element_type=jnp.float32)
            + jnp.einsum("hqk,qhd->khd", grad_scores, inputs_h, preferred_element_type=jnp.float32)
        )
        grad_in = grad_own.astype(jnp.float32) + through.reshape(seq_len, half_width)
        return grad_in.astype(jnp.bfloat16)

    def resting(grad_full, grad_own, inputs, probs, probs_low):
        return jnp.zeros((seq_len, half_width), jnp.bfloat16)

    carried_state = jnp.zeros((seq_len, half_width), jnp.bfloat16)
    out_list = []
    grad_list = []
    total_steps = micro_count + section_count - 1
    for step_number in range(total_steps):
        micro_index = step_number - (section_count - 1 - section_index)
        active = (micro_index >= 0) & (micro_index < micro_count)
        slot_index = jnp.clip(micro_index, 0, micro_count - 1)
        from_top = lax.dynamic_index_in_dim(top_cotangent, slot_index, 0, keepdims=False)
        incoming = jnp.where(section_index == section_count - 1, from_top, carried_state)
        grad_full = lax.all_gather(incoming, "mp", axis=1, tiled=True)
        inputs_now = lax.dynamic_index_in_dim(every_layer_input, slot_index, 0, keepdims=False)
        probs_now = lax.dynamic_index_in_dim(probs_all, slot_index, 0, keepdims=False)
        low_now = lax.dynamic_index_in_dim(low_all, slot_index, 0, keepdims=False)
        grad_in = lax.cond(
            active, layer_back, resting, grad_full, incoming, inputs_now, probs_now, low_now
        )
        out_list.append(grad_in)
        grad_list.append(grad_full)
        if step_number < total_steps - 1:
            carried_state = jax.tree.map(
                lambda part, own: part.astype(own.dtype),
                passed_along(for_sending(grad_in), "section", -1),
                grad_in,
            )
    offset = section_count - 1 - section_index
    out_store = lax.dynamic_slice_in_dim(jnp.stack(out_list), offset, micro_count, 0)
    grad_store = lax.dynamic_slice_in_dim(jnp.stack(grad_list), offset, micro_count, 0)
    summed_weight = lax.psum_scatter(
        jnp.einsum(
            "mtf,mta->fa", grad_store, attend_store, preferred_element_type=jnp.float32
        ).astype(jnp.bfloat16),
        "samples",
        scatter_dimension=0,
        tiled=True,
    ).astype(jnp.float32)
    region_count = seq_len // 2
    rank_in_region = jnp.cumsum(region_mask) - 1
    select = (
        (rank_in_region[None, :] == jnp.arange(region_count)[:, None]) & (region_mask[None, :] > 0)
    ).astype(jnp.bfloat16)
    tiles = jnp.einsum("at,mtd->mad", select, out_store, preferred_element_type=jnp.float32).astype(
        jnp.bfloat16
    )
    shard_index = lax.axis_index("samples")
    my_partners = lax.dynamic_slice_in_dim(
        partner_samples, shard_index * micro_count, micro_count, 0
    )
    shard_count = lax.axis_size("samples")
    dest_shard = my_partners // micro_count
    dest_slot = my_partners % micro_count
    route = (
        (dest_shard[:, None, None] == jnp.arange(shard_count)[None, :, None])
        & (dest_slot[:, None, None] == jnp.arange(micro_count)[None, None, :])
    ).astype(jnp.bfloat16)
    outgoing = jnp.einsum("mku,mad->kuad", route, tiles, preferred_element_type=jnp.float32).astype(
        jnp.bfloat16
    )
    arrived = lax.all_to_all(outgoing, "samples", split_axis=0, concat_axis=0, tiled=True)
    ones_row = jnp.ones((shard_count,), jnp.bfloat16)
    received = jnp.einsum(
        "k,kuad->uad", ones_row, arrived, preferred_element_type=jnp.float32
    ).astype(jnp.bfloat16)
    placed = jnp.einsum("at,mad->mtd", select, received, preferred_element_type=jnp.float32)
    kept = jnp.where(region_mask[None, :, None] > 0, jnp.zeros_like(out_store), out_store)
    site_cot = (kept.astype(jnp.float32) + placed).astype(jnp.bfloat16)
    cotangents = jnp.where(section_index == 0, site_cot, out_store)
    onehot = (spins[:, :, None] == jnp.arange(SPINS)[None, None, :]).astype(jnp.bfloat16)
    embed_term = jnp.einsum("mtv,mtd->vd", onehot, site_cot, preferred_element_type=jnp.float32)
    embed_term = jnp.where(section_index == 0, embed_term, jnp.zeros_like(embed_term))
    embed_grad = lax.psum(embed_term, ("samples", "section"))
    return (summed_weight[None], cotangents[None], embed_grad)


def solution(mesh):
    in_specs = (
        P("section", ("groups", "samples"), None, "mp"),
        P(("groups", "samples"), None, "mp"),
        P("section", "samples", "mp"),
        P("section", None, None),
        P(),
        P("groups"),
        P(("groups", "samples"), None),
    )
    out_specs = (
        P(("groups", "section"), "samples", "mp"),
        P("section", ("groups", "samples"), None, "mp"),
        P("groups", "mp"),
    )
    return jax.shard_map(local, mesh=mesh, in_specs=in_specs, out_specs=out_specs, check_vma=False)
```

profile of v0, /device:TPU:0, one launch (start us, length us, event | category | flops | bytes accessed | tf_op | source)
XLA Modules:
  0.0 230.9 jit_solution(3617918182335922141)
XLA Ops:
  7.2 0.7 all-gather.4.cloned.1.call-update
  8.0 1.1 fusion.20
  9.2 1.0 copy.68
  10.4 2.5 %all-gather = bf16[1,128,2048]{2,1,0:T(8,128)(2,1)S(1)} all-gather(bf16[1,128,1024]{2,1,0:T(8,128)(2,1)} %param.8), channel_id=2, replica_groups=mesh['groups'=2,'samples'=8,'section'=1,'mp'=2] {'mp'}, dimensions={2}, use_global_device_ids=true | all-gather | bytes 786432 | tf_op jit(solution)/shard_map/all_gather | solution.py:100
  13.0 0.4 fusion.78
  13.3 0.5 convolution_convert_fusion
  13.9 3.2 %convert_bitcast_fusion = bf16[2048,1024]{0,1:T(8,128)(2,1)} fusion(bf16[128,1024]{0,1:T(8,128)(2,1)S(1)} %bitcast.106, bf16[1,128,2048]{2,1,0:T(8,128)(2,1)S(1)} %all-gather), kind=kOutput, calls=%fused_computation.3 | convolution fusion | flops 538968064 | bytes 4980736 | tf_op jit(solution)/shard_map/mtf,mta->fa/dot_general | solution.py:119
  17.3 0.4 copy-done.1
  18.0 0.6 dynamic_slice.12
  18.6 0.6 fusion.61
  19.3 66.3 %all-gather.4.cloned.1.call-done = bf16[1,2048,1024]{2,1,0:T(8,128)(2,1)} async-done(((bf16[1,256,1024]{2,1,0:T(8,128)(2,1)}), bf16[1,2048,1024]{2,1,0:T(8,128)(2,1)}) %all-gather.4.cloned.1.call-update) | async-done | bytes 4194320 | tf_op jit(solution)/shard_map/all_gather | solution.py:47
  85.6 2.9 %fusion.14 = bf16[16,8,8,128]{3,2,1,0:T(8,128)(2,1)S(1)} fusion(bf16[1,2048,1024]{2,1,0:T(8,128)(2,1)} %all-gather.4.cloned.1.call-done, bf16[1,128,2048]{2,1,0:T(8,128)(2,1)S(1)} %all-gather), kind=kOutput, calls=%fused_computation.19 | convolution fusion | flops 537001984 | bytes 4980736 | tf_op jit(solution)/shard_map/cond/branch_1_fun/dot_general | solution.py:68
  88.6 0.3 multiply_reduce_fusion
  89.0 0.3 fusion.81
  89.5 0.5 fusion.5
  90.3 1.2 fusion.23
  91.5 3.7 %all-to-all-start = ((bf16[8,1,64,1024]{3,2,1,0:T(8,128)(2,1)}), bf16[8,1,64,1024]{3,2,1,0:T(8,128)(2,1)S(1)}, u32[]{:S(2)}, u32[]{:S(2)}) async-start(bf16[8,1,64,1024]{3,2,1,0:T(8,128)(2,1)} %fusion.23), calls=%async_computation.1 | async-start | bytes 2097152 | tf_op jit(solution)/shard_map/all_to_all | solution.py:148
  95.3 103.4 %reduce-scatter.2.cloned.1.call-done = bf16[256,1024]{0,1:T(8,128)(2,1)} async-done(((bf16[2048,1024]{0,1:T(8,128)(2,1)}), bf16[256,1024]{0,1:T(8,128)(2,1)}) %reduce-scatter.2.cloned.1.call-update) | async-done | bytes 524304 | tf_op jit(solution)/shard_map/reduce_scatter | solution.py:118
  198.7 1.1 bitcast_convert_fusion
  199.8 1.3 copy.59
  201.1 0.8 fusion.24
  201.9 0.3 fusion.10
  202.3 20.9 %psum.7 = f32[2,1024]{1,0:T(2,128)} all-reduce(f32[2,1024]{1,0:T(2,128)S(1)} %fusion.35), channel_id=1, replica_groups=mesh['groups'=2,'samples'=8,'section'=1,'mp'=2] {'samples','section'}, use_global_device_ids=true, to_apply=%region_5.6 | all-reduce | flops 2048 | bytes 16384 | tf_op jit(solution)/shard_map/psum | solution.py:160
  223.2 0.8 copy.60
  (25 shorter events, 1.8 us)
Async XLA Ops:
  7.2 78.5 %all-gather.4.cloned.1.call-start = ((), (), s32[]{:S(2)}) async-start(), calls=%async_computation.3 | async-start | bytes 4718592 | tf_op jit(solution)/shard_map/all_gather | solution.py:47
  7.9 190.8 %reduce-scatter.2.cloned.1.call-start = ((), (), s32[]{:S(2)}) async-start(), calls=%async_computation.2 | async-start | bytes 4718592 | tf_op jit(solution)/shard_map/reduce_scatter | solution.py:118
  13.9 3.2 %copy-start = (bf16[1,128,1024]{2,1,0:T(8,128)(2,1)S(1)}, bf16[1,128,1024]{2,1,0:T(8,128)(2,1)}, u32[]{:S(2)}) copy-start(bf16[1,128,1024]{2,1,0:T(8,128)(2,1)} %param.8) | copy-start | bytes 786436
  17.0 0.7 copy-start.1
  17.0 0.9 copy-start.3
  91.5 110.6 %copy-start.2 = (s32[1,128]{1,0:T(1,128)S(1)}, s32[1,128]{1,0:T(1,128)}, u32[]{:S(2)}) copy-start(s32[1,128]{1,0:T(1,128)} %param.13) | copy-start | bytes 1540
  91.5 109.6 %all-to-all-start = ((bf16[8,1,64,1024]{3,2,1,0:T(8,128)(2,1)}), bf16[8,1,64,1024]{3,2,1,0:T(8,128)(2,1)S(1)}, u32[]{:S(2)}, u32[]{:S(2)}) async-start(bf16[8,1,64,1024]{3,2,1,0:T(8,128)(2,1)} %fusion.23), calls=%async_computation.1 | async-start | bytes 2097152 | tf_op jit(solution)/shard_map/all_to_all | solution.py:148
Sparse Core Ops, SparseCore 0:
  10.1 75.4 all-gather.3
  89.3 109.3 reduce-scatter.1
where the time goes:
time: 231 us
  waiting for transfers between devices  170 us (74%)
  blocking collectives  23.4 us (10%)
  between operations  14.2 us (6%)
  matrix products  10.9 us (5%)
  local copies, waits for them, and re-layouts  4.81 us (2%)
  starting transfers between devices  3.76 us (2%)
  other arithmetic  3.48 us (2%)
    reduce_scatter x1, waiting for transfers between devices, local(): lax.psum_scatter(jnp.einsum('mtf,mta->fa', grad_store, attend_store, pref...  103 us
    all_gather x1, waiting for transfers between devices, local(): weights = lax.all_gather(layer_weights[0], 'samples', axis=0, tiled=True)  66.3 us
    psum x1, blocking collectives, local(): embed_grad = lax.psum(embed_term, ('samples', 'section'))  20.9 us
  transfers between devices with their start and end apart: 3, of which 2 were waited for; matrix products, arithmetic and copies ran while one was open for 7% of the time, Pallas kernels for 0%

commit v1 on v0

--- a/solution.py
+++ b/solution.py
@@ -1,6 +1,8 @@
 import jax
 import jax.numpy as jnp
 from jax import lax
+from jax.experimental import pallas as pl
+from jax.experimental.pallas import tpu as pltpu
 from jax.sharding import PartitionSpec as P
 
 HEAD = 128
@@ -161,6 +163,346 @@
     return (summed_weight[None], cotangents[None], embed_grad)
 
 
+NZ = 4
+MESH = pl.DeviceIdType.MESH
+F32 = jnp.float32
+BF = jnp.bfloat16
+
+
+def dot(a, b, ca=1, cb=0):
+    return lax.dot_general(a, b, (((ca,), (cb,)), ((), ())), preferred_element_type=F32)
+
+
+def kernel(
+    x_ref, g_ref, w_ref, layout_ref, mask_ref, partner_ref, spin_ref,
+    wg_ref, cot_ref, emb_ref,
+    gq, w2, pf, pb, rl, rr, att, probs, ga, g0, tile, swz, xsend, xrecv,
+    spall, embs, wsend, wrecv, wown,
+    gq_s, gq_r, gf_s, gf_r, w_s, w_r, sp_s, sp_r, at_s, at_r, rs_s, rs_r,
+    sw_s, sw_r, xs_s, xs_r, em_s, em_r, wr_s, wr_r,
+):
+    s = lax.axis_index("samples")
+    m = lax.axis_index("mp")
+    z = s // 2
+    x = s % 2
+    scale = 4.0 / HEAD
+    tokens, width = x_ref.shape
+    heads = width // HEAD
+    rows = w_ref.shape[0]
+    sibling = {"mp": 1 - m}
+    beside = {"samples": 2 * z + 1 - x}
+
+    def rdma(src, dst, ss, rs, dev):
+        return pltpu.make_async_remote_copy(
+            src_ref=src, dst_ref=dst, send_sem=ss, recv_sem=rs, device_id=dev, device_id_type=MESH
+        )
+
+    sends = []
+
+    def send(cond, make):
+        if cond is None:
+            make().start()
+        else:
+            pl.when(cond)(lambda: make().start())
+        sends.append((cond, make))
+
+    def got(cond, dst, rs):
+        def wait():
+            rdma(dst, dst, rs, rs, sibling).wait_recv()
+
+        if cond is None:
+            wait()
+        else:
+            pl.when(cond)(wait)
+
+    barrier = pltpu.get_barrier_semaphore()
+    for k in range(1, 8):
+        pl.semaphore_signal(
+            barrier, inc=1, device_id={"samples": lax.rem(s + k, 8)}, device_id_type=MESH
+        )
+    pl.semaphore_signal(barrier, inc=1, device_id=sibling, device_id_type=MESH)
+    pl.semaphore_wait(barrier, 8)
+
+    half = width // 2
+    for j in range(2):
+        dz = 2 * m + j
+        for_me = dz == z
+        piece = g_ref.at[:, pl.ds(j * half, half)]
+        send(
+            jnp.logical_not(for_me),
+            lambda piece=piece, dz=dz, j=j: rdma(
+                piece, gq.at[z], gq_s.at[j], gq_r.at[z], {"samples": 2 * dz + x}
+            ),
+        )
+        send(
+            for_me,
+            lambda piece=piece, j=j: rdma(piece, gq.at[z], gq_s.at[j], gf_r.at[z], sibling),
+        )
+
+        @pl.when(for_me)
+        def _(j=j):
+            gq[z] = g_ref[:, pl.ds(j * half, half)]
+
+    send(None, lambda: rdma(w_ref, w2.at[x], w_s, w_r, beside))
+    for k in range(1, 8):
+        other = lax.rem(s + k, 8)
+        send(
+            None,
+            lambda k=k, other=other: rdma(
+                spin_ref, spall.at[s], sp_s.at[k], sp_r.at[s], {"samples": other}
+            ),
+        )
+    w2[x] = w_ref[...]
+    spall[s] = spin_ref[...]
+
+    qb = lax.broadcasted_iota(jnp.int32, (tokens, tokens), 0) // BLOCK
+    kb = lax.broadcasted_iota(jnp.int32, (tokens, tokens), 1) // BLOCK
+    linked = jnp.where(qb < kb, layout_ref[0, 1], layout_ref[1, 0])
+    allowed = (qb == kb) | (linked > 0)
+    for h in range(heads):
+        cols = pl.ds(h * HEAD, HEAD)
+        xh = x_ref[:, cols]
+        scores = jnp.where(allowed, dot(xh, xh, 1, 1) * scale, -jnp.inf)
+        expo = jnp.exp(scores - jnp.max(scores, axis=-1, keepdims=True))
+        p = expo / jnp.sum(expo, axis=-1, keepdims=True)
+        probs[h] = p
+        att[z, :, cols] = dot(p.astype(BF), xh).astype(BF)
+
+    def att_hop(k):
+        send(
+            (z < NZ - 1) & (z - k >= 0),
+            lambda: rdma(
+                att.at[z - k], att.at[z - k], at_s.at[0, k], at_r.at[0, k], {"samples": s + 2}
+            ),
+        )
+        send(
+            (z > 0) & (z + k <= NZ - 1),
+            lambda: rdma(
+                att.at[z + k], att.at[z + k], at_s.at[1, k], at_r.at[1, k], {"samples": s - 2}
+            ),
+        )
+
+    def att_wait(k):
+        got(z - 1 - k >= 0, att.at[0], at_r.at[0, k])
+        got(z + 1 + k <= NZ - 1, att.at[0], at_r.at[1, k])
+
+    att_hop(0)
+
+    first_core = m == z // 2
+    for zz in range(NZ):
+        near = first_core & (zz != z)
+        got(near, gq.at[zz], gq_r.at[zz])
+        send(near, lambda zz=zz: rdma(gq.at[zz], gq.at[zz], gf_s.at[zz], gf_r.at[zz], sibling))
+    for zz in range(NZ):
+        got(jnp.logical_not(first_core), gq.at[zz], gf_r.at[zz])
+    got(None, w2.at[0], w_r)
+    for d in (0, 3, 1, 2):
+        part = dot(gq[d, :, :rows], w2[0]) + dot(gq[d, :, rows:], w2[1])
+        pf[d] = part
+        pb[d] = part.astype(BF)
+
+    for d in range(NZ - 1):
+        e = NZ - 1 - d
+        relay = (z > d) & (z < NZ - 1)
+        got(relay, rl.at[d], rs_r.at[0, d])
+
+        @pl.when(relay)
+        def _(d=d):
+            pb[d] = (pf[d] + rl[d].astype(F32)).astype(BF)
+
+        send(
+            z > d,
+            lambda d=d: rdma(pb.at[d], rl.at[d], rs_s.at[0, d], rs_r.at[0, d], {"samples": s - 2}),
+        )
+        relay = (z < e) & (z > 0)
+        got(relay, rr.at[e], rs_r.at[1, e])
+
+        @pl.when(relay)
+        def _(e=e):
+            pb[e] = (pf[e] + rr[e].astype(F32)).astype(BF)
+
+        send(
+            z < e,
+            lambda e=e: rdma(pb.at[e], rr.at[e], rs_s.at[1, e], rs_r.at[1, e], {"samples": s + 2}),
+        )
+
+    att_wait(0)
+    att_hop(1)
+
+    for d in range(NZ - 1):
+        got((z == d), rl.at[d], rs_r.at[0, d])
+        got((z == d + 1), rr.at[d + 1], rs_r.at[1, d + 1])
+
+    @pl.when(z == 0)
+    def _():
+        ga[...] = (pf[0] + rl[0].astype(F32)).astype(BF)
+
+    @pl.when(z == NZ - 1)
+    def _():
+        ga[...] = (pf[NZ - 1] + rr[NZ - 1].astype(F32)).astype(BF)
+
+    for d in range(1, NZ - 1):
+
+        @pl.when(z == d)
+        def _(d=d):
+            ga[...] = (pf[d] + rl[d].astype(F32) + rr[d].astype(F32)).astype(BF)
+
+    for h in range(heads):
+        cols = pl.ds(h * HEAD, HEAD)
+        xh = x_ref[:, cols]
+        gh = ga[:, cols]
+        p = probs[h]
+        gp = dot(gh, xh, 1, 1)
+        gs = (p * (gp - jnp.sum(gp * p, axis=-1, keepdims=True))).astype(BF)
+        through = dot(p.astype(BF), gh, 0, 0) + scale * (dot(gs, xh) + dot(gs, xh, 0, 0))
+        g0[:, cols] = (g_ref[:, cols].astype(F32) + through).astype(BF)
+
+    mask = mask_ref[...]
+    tri = (
+        lax.broadcasted_iota(jnp.int32, (tokens, tokens), 0)
+        <= lax.broadcasted_iota(jnp.int32, (tokens, tokens), 1)
+    ).astype(F32).astype(BF)
+    mask_rows = jnp.broadcast_to(mask, (8, tokens)).astype(F32)
+    rank = dot(mask_rows.astype(BF), tri)[:1] - 1.0
+    region = tokens // 2
+    place = lax.broadcasted_iota(jnp.int32, (region, tokens), 0).astype(F32)
+    select = jnp.where((rank == place) & (mask > 0), 1.0, 0.0).astype(BF)
+    tile[...] = dot(select, g0[...]).astype(BF)
+    for k in range(1, NZ):
+        dz = lax.rem(z + k, NZ)
+        send(
+            None,
+            lambda k=k, dz=dz: rdma(
+                tile, swz.at[z], sw_s.at[k], sw_r.at[z], {"samples": 2 * dz + x}
+            ),
+        )
+    swz[z] = tile[...]
+
+    for k in range(1, 8):
+        other = lax.rem(s + k, 8)
+        got(None, spall.at[0], sp_r.at[other])
+    mine = partner_ref[s]
+    spins = jnp.where(mask > 0, spall[mine], spin_ref[...])
+    onehot = jnp.where(
+        spins == lax.broadcasted_iota(jnp.int32, (8, tokens), 0), 1.0, 0.0
+    ).astype(BF)
+    embs[s] = dot(onehot, g0[...])[:SPINS]
+    for k in range(1, 8):
+        other = lax.rem(s + k, 8)
+        send(
+            None,
+            lambda k=k, other=other: rdma(
+                embs.at[s], embs.at[s], em_s.at[k], em_r.at[s], {"samples": other}
+            ),
+        )
+
+    att_wait(1)
+    att_hop(2)
+    att_wait(2)
+    for c in range(4):
+        cols = pl.ds(c * 256, 256)
+        total = jnp.zeros((2 * rows, 256), F32)
+        for zz in range(NZ):
+            total += dot(gq[zz], att[zz, :, cols], 0, 0).astype(BF).astype(F32)
+
+        @pl.when(x == 0)
+        def _(cols=cols, total=total):
+            wown[:, cols] = total[:rows]
+            wsend[:, cols] = total[rows:].astype(BF)
+
+        @pl.when(x == 1)
+        def _(cols=cols, total=total):
+            wown[:, cols] = total[rows:]
+            wsend[:, cols] = total[:rows].astype(BF)
+
+    send(None, lambda: rdma(wsend, wrecv, wr_s, wr_r, beside))
+
+    for k in range(1, NZ):
+        got(None, swz.at[0], sw_r.at[lax.rem(z + k, NZ)])
+    theirs = partner_ref[2 * z + 1 - x]
+    xsend[...] = swz[theirs // 2]
+    send(None, lambda: rdma(xsend, xrecv, xs_s, xs_r, beside))
+    same = jnp.where(mine % 2 == x, 1, 0)
+    local_rows = swz[mine // 2]
+    eye = lax.broadcasted_iota(jnp.int32, (tokens, tokens), 0) == lax.broadcasted_iota(
+        jnp.int32, (tokens, tokens), 1
+    )
+    keep = jnp.where(eye & (mask == 0), 1.0, 0.0).astype(BF)
+    kept = dot(keep, g0[...])
+    for k in range(1, 8):
+        got(None, embs.at[0], em_r.at[lax.rem(s + k, 8)])
+    total = embs[0]
+    for k in range(1, 8):
+        total += embs[k]
+    emb_ref[...] = total
+    got(None, xrecv, xs_r)
+    chosen = jnp.where(same > 0, local_rows, xrecv[...])
+    cot_ref[...] = (kept + dot(select, chosen, 0, 0)).astype(BF)
+    got(None, wrecv, wr_r)
+    wg_ref[...] = wown[...] + wrecv[...].astype(F32)
+
+    for cond, make in sends:
+        if cond is None:
+            make().wait_send()
+        else:
+            pl.when(cond)(lambda make=make: make().wait_send())
+
+
+def one_layer(
+    stored_inputs, top_cotangent, layer_weights, block_layout, region_mask, partner_samples, spins
+):
+    tokens, width = stored_inputs.shape[2:]
+    rows = layer_weights.shape[1]
+    vmem = pl.BlockSpec(memory_space=pltpu.VMEM)
+    smem = pl.BlockSpec(memory_space=pltpu.SMEM)
+    region = tokens // 2
+    dma = pltpu.SemaphoreType.DMA
+    shapes = [
+        ((NZ, tokens, width // 2), BF),
+        ((2, rows, width), BF),
+        ((NZ, tokens, width), F32),
+        ((NZ, tokens, width), BF),
+        ((NZ, tokens, width), BF),
+        ((NZ, tokens, width), BF),
+        ((NZ, tokens, width), BF),
+        ((width // HEAD, tokens, tokens), F32),
+        ((tokens, width), BF),
+        ((tokens, width), BF),
+        ((region, width), BF),
+        ((NZ, region, width), BF),
+        ((region, width), BF),
+        ((region, width), BF),
+        ((8, 1, tokens), jnp.int32),
+        ((8, SPINS, width), F32),
+        ((rows, width), BF),
+        ((rows, width), BF),
+        ((rows, width), F32),
+    ]
+    sems = [
+        dma((2,)), dma((NZ,)), dma((NZ,)), dma((NZ,)), dma, dma, dma((8,)), dma((8,)),
+        dma((2, 3)), dma((2, 3)), dma((2, NZ)), dma((2, NZ)), dma((NZ,)), dma((NZ,)),
+        dma, dma, dma((8,)), dma((8,)), dma, dma,
+    ]
+    wg, cot, emb = pl.pallas_call(
+        kernel,
+        out_shape=[
+            jax.ShapeDtypeStruct((rows, width), F32),
+            jax.ShapeDtypeStruct((tokens, width), BF),
+            jax.ShapeDtypeStruct((SPINS, width), F32),
+        ],
+        in_specs=[vmem, vmem, vmem, smem, vmem, smem, vmem],
+        out_specs=[vmem] * 3,
+        scratch_shapes=[pltpu.VMEM(a, b) for a, b in shapes] + sems,
+        compiler_params=pltpu.CompilerParams(
+            collective_id=0, has_side_effects=True, vmem_limit_bytes=48 * 1024 * 1024
+        ),
+    )(
+        stored_inputs[0, 0], top_cotangent[0], layer_weights[0], block_layout[0],
+        region_mask[None], partner_samples, spins,
+    )
+    return wg[None], cot[None, None], emb
+
+
 def solution(mesh):
     in_specs = (
         P("section", ("groups", "samples"), None, "mp"),
@@ -176,4 +518,6 @@
         P("section", ("groups", "samples"), None, "mp"),
         P("groups", "mp"),
     )
-    return jax.shard_map(local, mesh=mesh, in_specs=in_specs, out_specs=out_specs, check_vma=False)
+    small = mesh.shape["samples"] == 8 and mesh.shape["section"] == 1 and mesh.shape["mp"] == 2
+    body = one_layer if small else local
+    return jax.shard_map(body, mesh=mesh, in_specs=in_specs, out_specs=out_specs, check_vma=False)

time: 231 us -> 83 us (0.36)
  waiting for transfers between devices: 170 us -> 0 us
  Pallas kernels: 0 us -> 76.2 us
  blocking collectives: 23.4 us -> 0 us
  between operations: 14.2 us -> 0.68 us
  matrix products: 10.9 us -> 0 us
  starting transfers between devices: 3.76 us -> 0 us
  other arithmetic: 3.48 us -> 0 us
    reduce_scatter x1 -> x0, waiting for transfers between devices: 103 us -> none  [local(): lax.psum_scatter(jnp.einsum('mtf,mta->fa', grad_store, attend_store, pref...]
    pallas_call x0 -> x1, Pallas kernels: none -> 76.2 us  [one_layer(): pl.pallas_call(kernel, out_shape=[jax.ShapeDtypeStruct((rows, width), F32...]
    all_gather x1 -> x0, waiting for transfers between devices: 66.3 us -> none  [local(): weights = lax.all_gather(layer_weights[0], 'samples', axis=0, tiled=True)]
    psum x1 -> x0, blocking collectives: 20.9 us -> none  [local(): embed_grad = lax.psum(embed_term, ('samples', 'section'))]
    dot_general x12 -> x0, matrix products: 10.5 us -> none  [the longest x1 3.16 us: local(): jnp.einsum('mtf,mta->fa', grad_store, attend_store, preferred_element_typ...]
    all_to_all x1 -> x0, starting transfers between devices: 3.69 us -> none  [local(): lax.all_to_all(outgoing, 'samples', split_axis=0, concat_axis=0, tiled=True)]
    all_gather x1 -> x0, blocking collectives: 2.51 us -> none  [local(): grad_full = lax.all_gather(incoming, 'mp', axis=1, tiled=True)]
    unnamed x12 -> x17, local copies, waits for them, and re-layouts: 3.77 us -> 5.89 us
  transfers between devices with their start and end apart: 3 -> 0, of which waited for: 2 -> 0; matrix products, arithmetic and copies ran while one was open for 7% -> 0% of each run, Pallas kernels for 0% -> 0%
where the time goes in v1:
time: 83 us; the launch traced here: 82.7 us
  Pallas kernels  76.2 us (92%)
  local copies, waits for them, and re-layouts  5.89 us (7%)
    pallas_call x1, Pallas kernels, one_layer(): pl.pallas_call(kernel, out_shape=[jax.ShapeDtypeStruct((rows, width), F32...  76.2 us
    unnamed x17, local copies, waits for them, and re-layouts  5.89 us

profile of v1, /device:TPU:0, one launch (start us, length us, event | category | flops | bytes accessed | tf_op | source)
XLA Modules:
  0.0 82.7 jit_solution(14263092198333614525)
XLA Ops:
  0.6 0.0 copy-start.5
  0.6 0.0 copy-start.6
  0.7 0.0 copy-start.3
  0.7 0.0 copy-start.4
  0.7 0.6 copy-done.5
  1.3 0.0 copy-done.6
  1.3 0.0 copy-done.3
  1.3 0.0 copy-done.4
  1.3 0.0 copy-start
  1.3 1.0 %copy-done = bf16[1,256,1024]{2,1,0:T(8,128)(2,1)S(1)} copy-done((bf16[1,256,1024]{2,1,0:T(8,128)(2,1)S(1)}, bf16[1,256,1024]{2,1,0:T(8,128)(2,1)}, u32[]{:S(2)}) %copy-start) | copy-done | bytes 524312
  2.4 0.0 copy-start.1
  2.4 0.9 %copy-done.1 = bf16[1,1,128,1024]{3,2,1,0:T(8,128)(2,1)S(1)} copy-done((bf16[1,1,128,1024]{3,2,1,0:T(8,128)(2,1)S(1)}, bf16[1,1,128,1024]{3,2,1,0:T(8,128)(2,1)}, u32[]{:S(2)}) %copy-start.1) | copy-done | bytes 262168
  3.3 0.0 copy-start.2
  3.3 0.9 %copy-done.2 = bf16[1,128,1024]{2,1,0:T(8,128)(2,1)S(1)} copy-done((bf16[1,128,1024]{2,1,0:T(8,128)(2,1)S(1)}, bf16[1,128,1024]{2,1,0:T(8,128)(2,1)}, u32[]{:S(2)}) %copy-start.2) | copy-done | bytes 262168
  4.3 76.2 %shard_map.94 = (f32[256,1024]{1,0:T(8,128)S(1)}, bf16[128,1024]{1,0:T(8,128)(2,1)S(1)}, f32[2,1024]{1,0:T(2,128)S(1)}) custom-call(bf16[128,1024]{1,0:T(8,128)(2,1)S(1)} %bitcast.10, bf16[128,1024]{1,0:T(8,128)(2,1)S(1)} %bitcast.11, bf16[256,1024]{1,0:T(8,128)(2,1)S(1)} %bitcast.8, s32[2,2]{1,0:T(2,128)S(1)} %bitcast.12, s32[1,128]{1,0:T(1,128)S(1)} %bitcast.13, ...), custom_call_target="tpu_custom_call" | custom-call | tf_op jit(solution)/shard_map/pallas_call | solution.py:486
  80.5 1.0 %copy.13 = f32[1,256,1024]{2,1,0:T(8,128)} copy(f32[1,256,1024]{2,1,0:T(8,128)S(1)} %bitcast.7) | data formatting | bytes 2097152
  81.4 0.7 copy.14
  82.1 0.6 copy.15
Async XLA Ops:
  0.6 0.7 copy-start.5
  0.6 0.7 copy-start.6
  0.7 0.7 copy-start.3
  0.7 0.7 copy-start.4
  1.3 1.0 %copy-start = (bf16[1,256,1024]{2,1,0:T(8,128)(2,1)S(1)}, bf16[1,256,1024]{2,1,0:T(8,128)(2,1)}, u32[]{:S(2)}) copy-start(bf16[1,256,1024]{2,1,0:T(8,128)(2,1)} %param.9) | copy-start | bytes 1572868
  2.4 0.9 %copy-start.1 = (bf16[1,1,128,1024]{3,2,1,0:T(8,128)(2,1)S(1)}, bf16[1,1,128,1024]{3,2,1,0:T(8,128)(2,1)}, u32[]{:S(2)}) copy-start(bf16[1,1,128,1024]{3,2,1,0:T(8,128)(2,1)} %param.7) | copy-start | bytes 786436
  3.3 0.9 %copy-start.2 = (bf16[1,128,1024]{2,1,0:T(8,128)(2,1)S(1)}, bf16[1,128,1024]{2,1,0:T(8,128)(2,1)}, u32[]{:S(2)}) copy-start(bf16[1,128,1024]{2,1,0:T(8,128)(2,1)} %param.8) | copy-start | bytes 786436

commit v2 on v1

--- a/solution.py
+++ b/solution.py
@@ -174,11 +174,11 @@
 
 
 def kernel(
-    x_ref, g_ref, w_ref, layout_ref, mask_ref, partner_ref, spin_ref,
+    x_hbm, g_hbm, w_hbm, layout_ref, mask_ref, partner_ref, spin_ref,
     wg_ref, cot_ref, emb_ref,
-    gq, w2, pf, pb, rl, rr, att, probs, ga, g0, tile, swz, xsend, xrecv,
+    x_ref, g_ref, gq, w2, pf, pb, rl, rr, att, probs, ga, g0, tile, swz, xsend, xrecv,
     spall, embs, wsend, wrecv, wown,
-    gq_s, gq_r, gf_s, gf_r, w_s, w_r, sp_s, sp_r, at_s, at_r, rs_s, rs_r,
+    in_s, gq_s, gq_r, gf_s, gf_r, w_s, w_r, sp_s, sp_r, at_s, at_r, rs_s, rs_r,
     sw_s, sw_r, xs_s, xs_r, em_s, em_r, wr_s, wr_r,
 ):
     s = lax.axis_index("samples")
@@ -188,7 +188,8 @@
     scale = 4.0 / HEAD
     tokens, width = x_ref.shape
     heads = width // HEAD
-    rows = w_ref.shape[0]
+    rows = w_hbm.shape[0]
+    half = width // 2
     sibling = {"mp": 1 - m}
     beside = {"samples": 2 * z + 1 - x}
 
@@ -215,6 +216,13 @@
         else:
             pl.when(cond)(wait)
 
+    loads = [
+        pltpu.make_async_copy(g_hbm, g_ref, in_s.at[0]),
+        pltpu.make_async_copy(w_hbm, w2.at[x], in_s.at[1]),
+        pltpu.make_async_copy(x_hbm, x_ref, in_s.at[2]),
+    ]
+    for load in loads:
+        load.start()
     barrier = pltpu.get_barrier_semaphore()
     for k in range(1, 8):
         pl.semaphore_signal(
@@ -223,7 +231,7 @@
     pl.semaphore_signal(barrier, inc=1, device_id=sibling, device_id_type=MESH)
     pl.semaphore_wait(barrier, 8)
 
-    half = width // 2
+    loads[0].wait()
     for j in range(2):
         dz = 2 * m + j
         for_me = dz == z
@@ -243,7 +251,10 @@
         def _(j=j):
             gq[z] = g_ref[:, pl.ds(j * half, half)]
 
-    send(None, lambda: rdma(w_ref, w2.at[x], w_s, w_r, beside))
+    loads[1].wait()
+    for c in range(2):
+        block = w2.at[x, :, pl.ds(c * half, half)]
+        send(None, lambda block=block, c=c: rdma(block, block, w_s.at[c], w_r.at[c], beside))
     for k in range(1, 8):
         other = lax.rem(s + k, 8)
         send(
@@ -252,9 +263,9 @@
                 spin_ref, spall.at[s], sp_s.at[k], sp_r.at[s], {"samples": other}
             ),
         )
-    w2[x] = w_ref[...]
     spall[s] = spin_ref[...]
 
+    loads[2].wait()
     qb = lax.broadcasted_iota(jnp.int32, (tokens, tokens), 0) // BLOCK
     kb = lax.broadcasted_iota(jnp.int32, (tokens, tokens), 1) // BLOCK
     linked = jnp.where(qb < kb, layout_ref[0, 1], layout_ref[1, 0])
@@ -295,67 +306,100 @@
         send(near, lambda zz=zz: rdma(gq.at[zz], gq.at[zz], gf_s.at[zz], gf_r.at[zz], sibling))
     for zz in range(NZ):
         got(jnp.logical_not(first_core), gq.at[zz], gf_r.at[zz])
-    got(None, w2.at[0], w_r)
-    for d in (0, 3, 1, 2):
-        part = dot(gq[d, :, :rows], w2[0]) + dot(gq[d, :, rows:], w2[1])
-        pf[d] = part
-        pb[d] = part.astype(BF)
-
-    for d in range(NZ - 1):
-        e = NZ - 1 - d
-        relay = (z > d) & (z < NZ - 1)
-        got(relay, rl.at[d], rs_r.at[0, d])
-
-        @pl.when(relay)
-        def _(d=d):
-            pb[d] = (pf[d] + rl[d].astype(F32)).astype(BF)
-
-        send(
-            z > d,
-            lambda d=d: rdma(pb.at[d], rl.at[d], rs_s.at[0, d], rs_r.at[0, d], {"samples": s - 2}),
-        )
-        relay = (z < e) & (z > 0)
-        got(relay, rr.at[e], rs_r.at[1, e])
-
-        @pl.when(relay)
-        def _(e=e):
-            pb[e] = (pf[e] + rr[e].astype(F32)).astype(BF)
-
-        send(
-            z < e,
-            lambda e=e: rdma(pb.at[e], rr.at[e], rs_s.at[1, e], rs_r.at[1, e], {"samples": s + 2}),
-        )
-
+
+    def partials(c):
+        got(None, w2.at[0, :, pl.ds(c * half, half)], w_r.at[c])
+        cols = pl.ds(c * half, half)
+        for d in range(NZ):
+            part = dot(gq[d, :, :rows], w2[0, :, cols]) + dot(gq[d, :, rows:], w2[1, :, cols])
+            pf[c, d] = part
+            pb[c, d] = part.astype(BF)
+        for d in range(NZ - 1):
+            e = NZ - 1 - d
+            send(
+                z == NZ - 1,
+                lambda d=d: rdma(
+                    pb.at[c, d], rl.at[c, d], rs_s.at[0, c, d], rs_r.at[0, c, d], {"samples": s - 2}
+                ),
+            )
+            send(
+                z == 0,
+                lambda e=e: rdma(
+                    pb.at[c, e], rr.at[c, e], rs_s.at[1, c, e], rs_r.at[1, c, e], {"samples": s + 2}
+                ),
+            )
+
+    def relay_left(c, at, d):
+        here = z == at
+        got(here, rl.at[c, d], rs_r.at[0, c, d])
+
+        @pl.when(here)
+        def _():
+            pb[c, d] = (pf[c, d] + rl[c, d].astype(F32)).astype(BF)
+
+        send(
+            here,
+            lambda: rdma(
+                pb.at[c, d], rl.at[c, d], rs_s.at[0, c, d], rs_r.at[0, c, d], {"samples": s - 2}
+            ),
+        )
+
+    def relay_right(c, at, e):
+        here = z == at
+        got(here, rr.at[c, e], rs_r.at[1, c, e])
+
+        @pl.when(here)
+        def _():
+            pb[c, e] = (pf[c, e] + rr[c, e].astype(F32)).astype(BF)
+
+        send(
+            here,
+            lambda: rdma(
+                pb.at[c, e], rr.at[c, e], rs_s.at[1, c, e], rs_r.at[1, c, e], {"samples": s + 2}
+            ),
+        )
+
+    def relays_near(c):
+        relay_left(c, 2, 0)
+        relay_right(c, 1, 3)
+        relay_left(c, 2, 1)
+        relay_right(c, 1, 2)
+
+    def relays_far(c):
+        relay_left(c, 1, 0)
+        relay_right(c, 2, 3)
+
+    partials(0)
     att_wait(0)
     att_hop(1)
-
-    for d in range(NZ - 1):
-        got((z == d), rl.at[d], rs_r.at[0, d])
-        got((z == d + 1), rr.at[d + 1], rs_r.at[1, d + 1])
-
-    @pl.when(z == 0)
-    def _():
-        ga[...] = (pf[0] + rl[0].astype(F32)).astype(BF)
-
-    @pl.when(z == NZ - 1)
-    def _():
-        ga[...] = (pf[NZ - 1] + rr[NZ - 1].astype(F32)).astype(BF)
-
-    for d in range(1, NZ - 1):
-
-        @pl.when(z == d)
-        def _(d=d):
-            ga[...] = (pf[d] + rl[d].astype(F32) + rr[d].astype(F32)).astype(BF)
-
-    for h in range(heads):
-        cols = pl.ds(h * HEAD, HEAD)
-        xh = x_ref[:, cols]
-        gh = ga[:, cols]
-        p = probs[h]
-        gp = dot(gh, xh, 1, 1)
-        gs = (p * (gp - jnp.sum(gp * p, axis=-1, keepdims=True))).astype(BF)
-        through = dot(p.astype(BF), gh, 0, 0) + scale * (dot(gs, xh) + dot(gs, xh, 0, 0))
-        g0[:, cols] = (g_ref[:, cols].astype(F32) + through).astype(BF)
+    partials(1)
+    relays_near(0)
+    att_wait(1)
+    att_hop(2)
+    relays_far(0)
+    relays_near(1)
+
+    att_wait(2)
+    for c in range(4):
+        cols = pl.ds(c * 256, 256)
+        total = jnp.zeros((2 * rows, 256), F32)
+        for zz in range(NZ):
+            total += dot(gq[zz], att[zz, :, cols], 0, 0).astype(BF).astype(F32)
+
+        @pl.when(x == 0)
+        def _(cols=cols, total=total):
+            wown[:, cols] = total[:rows]
+            wsend[:, cols] = total[rows:].astype(BF)
+
+        @pl.when(x == 1)
+        def _(cols=cols, total=total):
+            wown[:, cols] = total[rows:]
+            wsend[:, cols] = total[:rows].astype(BF)
+
+    send(None, lambda: rdma(wsend, wrecv, wr_s, wr_r, beside))
+
+
+    relays_far(1)
 
     mask = mask_ref[...]
     tri = (
@@ -367,16 +411,44 @@
     region = tokens // 2
     place = lax.broadcasted_iota(jnp.int32, (region, tokens), 0).astype(F32)
     select = jnp.where((rank == place) & (mask > 0), 1.0, 0.0).astype(BF)
-    tile[...] = dot(select, g0[...]).astype(BF)
-    for k in range(1, NZ):
-        dz = lax.rem(z + k, NZ)
-        send(
-            None,
-            lambda k=k, dz=dz: rdma(
-                tile, swz.at[z], sw_s.at[k], sw_r.at[z], {"samples": 2 * dz + x}
-            ),
-        )
-    swz[z] = tile[...]
+
+    def backward(c):
+        for d in range(NZ - 1):
+            got((z == d), rl.at[c, d], rs_r.at[0, c, d])
+            got((z == d + 1), rr.at[c, d + 1], rs_r.at[1, c, d + 1])
+        for d in range(NZ):
+
+            @pl.when(z == d)
+            def _(d=d):
+                total = pf[c, d]
+                if d < NZ - 1:
+                    total += rl[c, d].astype(F32)
+                if d > 0:
+                    total += rr[c, d].astype(F32)
+                ga[...] = total.astype(BF)
+
+        for h in range(heads // 2):
+            cols = pl.ds(c * half + h * HEAD, HEAD)
+            xh = x_ref[:, cols]
+            gh = ga[:, h * HEAD : (h + 1) * HEAD]
+            p = probs[c * (heads // 2) + h]
+            gp = dot(gh, xh, 1, 1)
+            gs = (p * (gp - jnp.sum(gp * p, axis=-1, keepdims=True))).astype(BF)
+            through = dot(p.astype(BF), gh, 0, 0) + scale * (dot(gs, xh) + dot(gs, xh, 0, 0))
+            g0[:, cols] = (g_ref[:, cols].astype(F32) + through).astype(BF)
+        tile[c] = dot(select, g0[:, pl.ds(c * half, half)]).astype(BF)
+        for k in range(1, NZ):
+            dz = lax.rem(z + k, NZ)
+            send(
+                None,
+                lambda k=k, dz=dz: rdma(
+                    tile.at[c], swz.at[c, z], sw_s.at[c, k], sw_r.at[c, z], {"samples": 2 * dz + x}
+                ),
+            )
+        swz[c, z] = tile[c]
+
+    backward(0)
+    backward(1)
 
     for k in range(1, 8):
         other = lax.rem(s + k, 8)
@@ -396,34 +468,21 @@
             ),
         )
 
-    att_wait(1)
-    att_hop(2)
-    att_wait(2)
-    for c in range(4):
-        cols = pl.ds(c * 256, 256)
-        total = jnp.zeros((2 * rows, 256), F32)
-        for zz in range(NZ):
-            total += dot(gq[zz], att[zz, :, cols], 0, 0).astype(BF).astype(F32)
-
-        @pl.when(x == 0)
-        def _(cols=cols, total=total):
-            wown[:, cols] = total[:rows]
-            wsend[:, cols] = total[rows:].astype(BF)
-
-        @pl.when(x == 1)
-        def _(cols=cols, total=total):
-            wown[:, cols] = total[rows:]
-            wsend[:, cols] = total[:rows].astype(BF)
-
-    send(None, lambda: rdma(wsend, wrecv, wr_s, wr_r, beside))
-
-    for k in range(1, NZ):
-        got(None, swz.at[0], sw_r.at[lax.rem(z + k, NZ)])
+    def rows_from(c, which):
+        rows_now = swz[c, 0]
+        for zz in range(1, NZ):
+            rows_now = jnp.where(which == zz, swz[c, zz], rows_now)
+        return rows_now
+
     theirs = partner_ref[2 * z + 1 - x]
-    xsend[...] = swz[theirs // 2]
-    send(None, lambda: rdma(xsend, xrecv, xs_s, xs_r, beside))
+    for c in range(2):
+        for k in range(1, NZ):
+            got(None, swz.at[c, 0], sw_r.at[c, lax.rem(z + k, NZ)])
+        xsend[c] = rows_from(c, theirs // 2)
+        send(
+            None, lambda c=c: rdma(xsend.at[c], xrecv.at[c], xs_s.at[c], xs_r.at[c], beside)
+        )
     same = jnp.where(mine % 2 == x, 1, 0)
-    local_rows = swz[mine // 2]
     eye = lax.broadcasted_iota(jnp.int32, (tokens, tokens), 0) == lax.broadcasted_iota(
         jnp.int32, (tokens, tokens), 1
     )
@@ -435,11 +494,13 @@
     for k in range(1, 8):
         total += embs[k]
     emb_ref[...] = total
-    got(None, xrecv, xs_r)
-    chosen = jnp.where(same > 0, local_rows, xrecv[...])
-    cot_ref[...] = (kept + dot(select, chosen, 0, 0)).astype(BF)
     got(None, wrecv, wr_r)
     wg_ref[...] = wown[...] + wrecv[...].astype(F32)
+    for c in range(2):
+        cols = slice(c * half, (c + 1) * half)
+        got(None, xrecv.at[c], xs_r.at[c])
+        chosen = jnp.where(same > 0, rows_from(c, mine // 2), xrecv[c])
+        cot_ref[:, cols] = (kept[:, cols] + dot(select, chosen, 0, 0)).astype(BF)
 
     for cond, make in sends:
         if cond is None:
@@ -453,25 +514,29 @@
 ):
     tokens, width = stored_inputs.shape[2:]
     rows = layer_weights.shape[1]
+    hbm = pl.BlockSpec(memory_space=pltpu.HBM)
     vmem = pl.BlockSpec(memory_space=pltpu.VMEM)
     smem = pl.BlockSpec(memory_space=pltpu.SMEM)
     region = tokens // 2
     dma = pltpu.SemaphoreType.DMA
+    half = width // 2
     shapes = [
-        ((NZ, tokens, width // 2), BF),
+        ((tokens, width), BF),
+        ((tokens, width), BF),
+        ((NZ, tokens, half), BF),
         ((2, rows, width), BF),
-        ((NZ, tokens, width), F32),
-        ((NZ, tokens, width), BF),
-        ((NZ, tokens, width), BF),
-        ((NZ, tokens, width), BF),
+        ((2, NZ, tokens, half), F32),
+        ((2, NZ, tokens, half), BF),
+        ((2, NZ, tokens, half), BF),
+        ((2, NZ, tokens, half), BF),
         ((NZ, tokens, width), BF),
         ((width // HEAD, tokens, tokens), F32),
+        ((tokens, half), BF),
         ((tokens, width), BF),
-        ((tokens, width), BF),
-        ((region, width), BF),
-        ((NZ, region, width), BF),
-        ((region, width), BF),
-        ((region, width), BF),
+        ((2, region, half), BF),
+        ((2, NZ, region, half), BF),
+        ((2, region, half), BF),
+        ((2, region, half), BF),
         ((8, 1, tokens), jnp.int32),
         ((8, SPINS, width), F32),
         ((rows, width), BF),
@@ -479,9 +544,9 @@
         ((rows, width), F32),
     ]
     sems = [
-        dma((2,)), dma((NZ,)), dma((NZ,)), dma((NZ,)), dma, dma, dma((8,)), dma((8,)),
-        dma((2, 3)), dma((2, 3)), dma((2, NZ)), dma((2, NZ)), dma((NZ,)), dma((NZ,)),
-        dma, dma, dma((8,)), dma((8,)), dma, dma,
+        dma((3,)), dma((2,)), dma((NZ,)), dma((NZ,)), dma((NZ,)), dma((2,)), dma((2,)),
+        dma((8,)), dma((8,)), dma((2, 3)), dma((2, 3)), dma((2, 2, NZ)), dma((2, 2, NZ)),
+        dma((2, NZ)), dma((2, NZ)), dma((2,)), dma((2,)), dma((8,)), dma((8,)), dma, dma,
     ]
     wg, cot, emb = pl.pallas_call(
         kernel,
@@ -490,7 +555,7 @@
             jax.ShapeDtypeStruct((tokens, width), BF),
             jax.ShapeDtypeStruct((SPINS, width), F32),
         ],
-        in_specs=[vmem, vmem, vmem, smem, vmem, smem, vmem],
+        in_specs=[hbm, hbm, hbm, smem, vmem, smem, vmem],
         out_specs=[vmem] * 3,
         scratch_shapes=[pltpu.VMEM(a, b) for a, b in shapes] + sems,
         compiler_params=pltpu.CompilerParams(

time: 83 us -> 60.6 us (0.73)
  Pallas kernels: 76.2 us -> 53.8 us
    pallas_call x1, Pallas kernels: 76.2 us -> 53.8 us  [one_layer(): pl.pallas_call(kernel, out_shape=[jax.ShapeDtypeStruct((rows, width), F32...]
where the time goes in v2:
time: 60.6 us; the launch traced here: 60.4 us
  Pallas kernels  53.8 us (89%)
  local copies, waits for them, and re-layouts  5.89 us (10%)
  between operations  0.68 us (1%)
    pallas_call x1, Pallas kernels, one_layer(): pl.pallas_call(kernel, out_shape=[jax.ShapeDtypeStruct((rows, width), F32...  53.8 us
    unnamed x17, local copies, waits for them, and re-layouts  5.89 us

profile of v2, /device:TPU:0, one launch (start us, length us, event | category | flops | bytes accessed | tf_op | source)
XLA Modules:
  0.0 60.4 jit_solution(5634363525564063005)
XLA Ops:
  0.6 0.0 copy-start.5
  0.6 0.0 copy-start.6
  0.7 0.0 copy-start.3
  0.7 0.0 copy-start.4
  0.7 0.6 %copy-done.5 = s32[8]{0:T(128)S(1)} copy-done((s32[8]{0:T(128)S(1)}, s32[8]{0:T(128)}, u32[]{:S(2)}) %copy-start.5) | copy-done | bytes 56
  1.3 0.0 copy-done.6
  1.3 0.0 copy-done.3
  1.3 0.0 copy-done.4
  1.3 0.0 copy-start
  1.3 1.0 %copy-done = bf16[1,256,1024]{2,1,0:T(8,128)(2,1)S(1)} copy-done((bf16[1,256,1024]{2,1,0:T(8,128)(2,1)S(1)}, bf16[1,256,1024]{2,1,0:T(8,128)(2,1)}, u32[]{:S(2)}) %copy-start) | copy-done | bytes 524312
  2.4 0.0 copy-start.1
  2.4 0.9 %copy-done.1 = bf16[1,1,128,1024]{3,2,1,0:T(8,128)(2,1)S(1)} copy-done((bf16[1,1,128,1024]{3,2,1,0:T(8,128)(2,1)S(1)}, bf16[1,1,128,1024]{3,2,1,0:T(8,128)(2,1)}, u32[]{:S(2)}) %copy-start.1) | copy-done | bytes 262168
  3.3 0.0 copy-start.2
  3.3 0.9 %copy-done.2 = bf16[1,128,1024]{2,1,0:T(8,128)(2,1)S(1)} copy-done((bf16[1,128,1024]{2,1,0:T(8,128)(2,1)S(1)}, bf16[1,128,1024]{2,1,0:T(8,128)(2,1)}, u32[]{:S(2)}) %copy-start.2) | copy-done | bytes 262168
  4.3 53.8 %shard_map.94 = (f32[256,1024]{1,0:T(8,128)S(1)}, bf16[128,1024]{1,0:T(8,128)(2,1)S(1)}, f32[2,1024]{1,0:T(2,128)S(1)}) custom-call(bf16[128,1024]{1,0:T(8,128)(2,1)S(1)} %bitcast.10, bf16[128,1024]{1,0:T(8,128)(2,1)S(1)} %bitcast.11, bf16[256,1024]{1,0:T(8,128)(2,1)S(1)} %bitcast.8, s32[2,2]{1,0:T(2,128)S(1)} %bitcast.12, s32[1,128]{1,0:T(1,128)S(1)} %bitcast.13, ...), custom_call_target="tpu_custom_call" | custom-call | tf_op jit(solution)/shard_map/pallas_call | solution.py:551
  58.1 1.0 %copy.13 = f32[1,256,1024]{2,1,0:T(8,128)} copy(f32[1,256,1024]{2,1,0:T(8,128)S(1)} %bitcast.7) | data formatting | bytes 2097152
  59.1 0.7 %copy.14 = bf16[1,1,128,1024]{3,2,1,0:T(8,128)(2,1)} copy(bf16[1,1,128,1024]{3,2,1,0:T(8,128)(2,1)S(1)} %bitcast.9) | data formatting | bytes 524288
  59.8 0.6 copy.15
Async XLA Ops:
  0.6 0.7 %copy-start.5 = (s32[8]{0:T(128)S(1)}, s32[8]{0:T(128)}, u32[]{:S(2)}) copy-start(s32[8]{0:T(128)} %partner_ref.1) | copy-start | bytes 100
  0.6 0.7 %copy-start.6 = (s32[1,128]{1,0:T(1,128)S(1)}, s32[1,128]{1,0:T(1,128)}, u32[]{:S(2)}) copy-start(s32[1,128]{1,0:T(1,128)} %spin_ref.1) | copy-start | bytes 1540
  0.7 0.7 %copy-start.3 = (s32[1,2,2]{2,1,0:T(2,128)S(1)}, s32[1,2,2]{2,1,0:T(2,128)}, u32[]{:S(2)}) copy-start(s32[1,2,2]{2,1,0:T(2,128)} %param.10) | copy-start | bytes 52
  0.7 0.7 %copy-start.4 = (s32[128]{0:T(128)S(1)}, s32[128]{0:T(128)}, u32[]{:S(2)}) copy-start(s32[128]{0:T(128)} %param.11) | copy-start | bytes 1540
  1.3 1.0 %copy-start = (bf16[1,256,1024]{2,1,0:T(8,128)(2,1)S(1)}, bf16[1,256,1024]{2,1,0:T(8,128)(2,1)}, u32[]{:S(2)}) copy-start(bf16[1,256,1024]{2,1,0:T(8,128)(2,1)} %param.9) | copy-start | bytes 1572868
  2.4 0.9 %copy-start.1 = (bf16[1,1,128,1024]{3,2,1,0:T(8,128)(2,1)S(1)}, bf16[1,1,128,1024]{3,2,1,0:T(8,128)(2,1)}, u32[]{:S(2)}) copy-start(bf16[1,1,128,1024]{3,2,1,0:T(8,128)(2,1)} %param.7) | copy-start | bytes 786436
  3.3 0.9 %copy-start.2 = (bf16[1,128,1024]{2,1,0:T(8,128)(2,1)S(1)}, bf16[1,128,1024]{2,1,0:T(8,128)(2,1)}, u32[]{:S(2)}) copy-start(bf16[1,128,1024]{2,1,0:T(8,128)(2,1)} %param.8) | copy-start | bytes 786436

commit v3 on v2

--- a/solution.py
+++ b/solution.py
@@ -174,9 +174,9 @@
 
 
 def kernel(
-    x_hbm, g_hbm, w_hbm, layout_ref, mask_ref, partner_ref, spin_ref,
+    x_hbm, g_hbm, w_hbm, layout_hbm, mask_hbm, partner_hbm, spin_hbm,
     wg_ref, cot_ref, emb_ref,
-    x_ref, g_ref, gq, w2, pf, pb, rl, rr, att, probs, ga, g0, tile, swz, xsend, xrecv,
+    x_ref, g_ref, layout_ref, mask_ref, partner_ref, spin_ref, gq, w2, pf, pb, rl, rr, att, probs, ga, g0, swz, xsend, xrecv,
     spall, embs, wsend, wrecv, wown,
     in_s, gq_s, gq_r, gf_s, gf_r, w_s, w_r, sp_s, sp_r, at_s, at_r, rs_s, rs_r,
     sw_s, sw_r, xs_s, xs_r, em_s, em_r, wr_s, wr_r,
@@ -220,6 +220,10 @@
         pltpu.make_async_copy(g_hbm, g_ref, in_s.at[0]),
         pltpu.make_async_copy(w_hbm, w2.at[x], in_s.at[1]),
         pltpu.make_async_copy(x_hbm, x_ref, in_s.at[2]),
+        pltpu.make_async_copy(spin_hbm, spin_ref, in_s.at[3]),
+        pltpu.make_async_copy(layout_hbm, layout_ref, in_s.at[4]),
+        pltpu.make_async_copy(mask_hbm, mask_ref, in_s.at[5]),
+        pltpu.make_async_copy(partner_hbm, partner_ref, in_s.at[6]),
     ]
     for load in loads:
         load.start()
@@ -255,6 +259,7 @@
     for c in range(2):
         block = w2.at[x, :, pl.ds(c * half, half)]
         send(None, lambda block=block, c=c: rdma(block, block, w_s.at[c], w_r.at[c], beside))
+    loads[3].wait()
     for k in range(1, 8):
         other = lax.rem(s + k, 8)
         send(
@@ -266,6 +271,8 @@
     spall[s] = spin_ref[...]
 
     loads[2].wait()
+    for load in loads[4:]:
+        load.wait()
     qb = lax.broadcasted_iota(jnp.int32, (tokens, tokens), 0) // BLOCK
     kb = lax.broadcasted_iota(jnp.int32, (tokens, tokens), 1) // BLOCK
     linked = jnp.where(qb < kb, layout_ref[0, 1], layout_ref[1, 0])
@@ -277,27 +284,37 @@
         expo = jnp.exp(scores - jnp.max(scores, axis=-1, keepdims=True))
         p = expo / jnp.sum(expo, axis=-1, keepdims=True)
         probs[h] = p
-        att[z, :, cols] = dot(p.astype(BF), xh).astype(BF)
-
-    def att_hop(k):
+        within = pl.ds(h % (heads // 2) * HEAD, HEAD)
+        att[h // (heads // 2), z, :, within] = dot(p.astype(BF), xh).astype(BF)
+
+    def hop(buf, ss, rs, c, k):
         send(
             (z < NZ - 1) & (z - k >= 0),
             lambda: rdma(
-                att.at[z - k], att.at[z - k], at_s.at[0, k], at_r.at[0, k], {"samples": s + 2}
+                buf.at[c, z - k], buf.at[c, z - k], ss.at[0, c, k], rs.at[0, c, k],
+                {"samples": s + 2},
             ),
         )
         send(
             (z > 0) & (z + k <= NZ - 1),
             lambda: rdma(
-                att.at[z + k], att.at[z + k], at_s.at[1, k], at_r.at[1, k], {"samples": s - 2}
-            ),
-        )
-
-    def att_wait(k):
-        got(z - 1 - k >= 0, att.at[0], at_r.at[0, k])
-        got(z + 1 + k <= NZ - 1, att.at[0], at_r.at[1, k])
-
-    att_hop(0)
+                buf.at[c, z + k], buf.at[c, z + k], ss.at[1, c, k], rs.at[1, c, k],
+                {"samples": s - 2},
+            ),
+        )
+
+    def hop_wait(buf, rs, c, k):
+        got(z - 1 - k >= 0, buf.at[c, 0], rs.at[0, c, k])
+        got(z + 1 + k <= NZ - 1, buf.at[c, 0], rs.at[1, c, k])
+
+    def att_hop(c, k):
+        hop(att, at_s, at_r, c, k)
+
+    def att_wait(c, k):
+        hop_wait(att, at_r, c, k)
+
+    att_hop(0, 0)
+    att_hop(1, 0)
 
     first_core = m == z // 2
     for zz in range(NZ):
@@ -314,20 +331,21 @@
             part = dot(gq[d, :, :rows], w2[0, :, cols]) + dot(gq[d, :, rows:], w2[1, :, cols])
             pf[c, d] = part
             pb[c, d] = part.astype(BF)
-        for d in range(NZ - 1):
-            e = NZ - 1 - d
-            send(
-                z == NZ - 1,
-                lambda d=d: rdma(
-                    pb.at[c, d], rl.at[c, d], rs_s.at[0, c, d], rs_r.at[0, c, d], {"samples": s - 2}
-                ),
-            )
-            send(
-                z == 0,
-                lambda e=e: rdma(
-                    pb.at[c, e], rr.at[c, e], rs_s.at[1, c, e], rs_r.at[1, c, e], {"samples": s + 2}
-                ),
-            )
+
+    def end_sends(c, d):
+        e = NZ - 1 - d
+        send(
+            z == NZ - 1,
+            lambda: rdma(
+                pb.at[c, d], rl.at[c, d], rs_s.at[0, c, d], rs_r.at[0, c, d], {"samples": s - 2}
+            ),
+        )
+        send(
+            z == 0,
+            lambda: rdma(
+                pb.at[c, e], rr.at[c, e], rs_s.at[1, c, e], rs_r.at[1, c, e], {"samples": s + 2}
+            ),
+        )
 
     def relay_left(c, at, d):
         here = z == at
@@ -359,47 +377,54 @@
             ),
         )
 
-    def relays_near(c):
-        relay_left(c, 2, 0)
-        relay_right(c, 1, 3)
-        relay_left(c, 2, 1)
-        relay_right(c, 1, 2)
-
-    def relays_far(c):
+    def inner(c, d):
+        relay_left(c, 2, d)
+        relay_right(c, 1, NZ - 1 - d)
+
+    def outer(c):
         relay_left(c, 1, 0)
-        relay_right(c, 2, 3)
+        relay_right(c, 2, NZ - 1)
+
+    def weight_terms(c):
+        for q in range(half // 256):
+            cols = pl.ds(c * half + q * 256, 256)
+            total = jnp.zeros((2 * rows, 256), F32)
+            for zz in range(NZ):
+                total += dot(gq[zz], att[c, zz, :, pl.ds(q * 256, 256)], 0, 0).astype(BF).astype(F32)
+
+            @pl.when(x == 0)
+            def _(cols=cols, q=q, total=total):
+                wown[:, cols] = total[:rows]
+                wsend[c, :, pl.ds(q * 256, 256)] = total[rows:].astype(BF)
+
+            @pl.when(x == 1)
+            def _(cols=cols, q=q, total=total):
+                wown[:, cols] = total[rows:]
+                wsend[c, :, pl.ds(q * 256, 256)] = total[:rows].astype(BF)
+
+        send(None, lambda: rdma(wsend.at[c], wrecv.at[c], wr_s.at[c], wr_r.at[c], beside))
 
     partials(0)
-    att_wait(0)
-    att_hop(1)
+    end_sends(0, 0)
+    att_wait(0, 0)
+    att_hop(0, 1)
     partials(1)
-    relays_near(0)
-    att_wait(1)
-    att_hop(2)
-    relays_far(0)
-    relays_near(1)
-
-    att_wait(2)
-    for c in range(4):
-        cols = pl.ds(c * 256, 256)
-        total = jnp.zeros((2 * rows, 256), F32)
-        for zz in range(NZ):
-            total += dot(gq[zz], att[zz, :, cols], 0, 0).astype(BF).astype(F32)
-
-        @pl.when(x == 0)
-        def _(cols=cols, total=total):
-            wown[:, cols] = total[:rows]
-            wsend[:, cols] = total[rows:].astype(BF)
-
-        @pl.when(x == 1)
-        def _(cols=cols, total=total):
-            wown[:, cols] = total[rows:]
-            wsend[:, cols] = total[:rows].astype(BF)
-
-    send(None, lambda: rdma(wsend, wrecv, wr_s, wr_r, beside))
-
-
-    relays_far(1)
+    end_sends(1, 0)
+    for d in range(1, NZ - 1):
+        for c in range(2):
+            end_sends(c, d)
+    inner(0, 0)
+    inner(1, 0)
+    att_wait(0, 1)
+    att_hop(0, 2)
+    outer(0)
+    inner(0, 1)
+    outer(1)
+    inner(1, 1)
+    att_wait(1, 0)
+    att_hop(1, 1)
+    att_wait(0, 2)
+    weight_terms(0)
 
     mask = mask_ref[...]
     tri = (
@@ -436,19 +461,16 @@
             gs = (p * (gp - jnp.sum(gp * p, axis=-1, keepdims=True))).astype(BF)
             through = dot(p.astype(BF), gh, 0, 0) + scale * (dot(gs, xh) + dot(gs, xh, 0, 0))
             g0[:, cols] = (g_ref[:, cols].astype(F32) + through).astype(BF)
-        tile[c] = dot(select, g0[:, pl.ds(c * half, half)]).astype(BF)
-        for k in range(1, NZ):
-            dz = lax.rem(z + k, NZ)
-            send(
-                None,
-                lambda k=k, dz=dz: rdma(
-                    tile.at[c], swz.at[c, z], sw_s.at[c, k], sw_r.at[c, z], {"samples": 2 * dz + x}
-                ),
-            )
-        swz[c, z] = tile[c]
+        swz[c, z] = dot(select, g0[:, pl.ds(c * half, half)]).astype(BF)
+        hop(swz, sw_s, sw_r, c, 0)
 
     backward(0)
     backward(1)
+    att_wait(1, 1)
+    att_hop(1, 2)
+    for c in range(2):
+        hop_wait(swz, sw_r, c, 0)
+        hop(swz, sw_s, sw_r, c, 1)
 
     for k in range(1, 8):
         other = lax.rem(s + k, 8)
@@ -474,10 +496,14 @@
             rows_now = jnp.where(which == zz, swz[c, zz], rows_now)
         return rows_now
 
+    for c in range(2):
+        hop_wait(swz, sw_r, c, 1)
+        hop(swz, sw_s, sw_r, c, 2)
+    att_wait(1, 2)
+    weight_terms(1)
     theirs = partner_ref[2 * z + 1 - x]
     for c in range(2):
-        for k in range(1, NZ):
-            got(None, swz.at[c, 0], sw_r.at[c, lax.rem(z + k, NZ)])
+        hop_wait(swz, sw_r, c, 2)
         xsend[c] = rows_from(c, theirs // 2)
         send(
             None, lambda c=c: rdma(xsend.at[c], xrecv.at[c], xs_s.at[c], xs_r.at[c], beside)
@@ -494,8 +520,10 @@
     for k in range(1, 8):
         total += embs[k]
     emb_ref[...] = total
-    got(None, wrecv, wr_r)
-    wg_ref[...] = wown[...] + wrecv[...].astype(F32)
+    for c in range(2):
+        cols = slice(c * half, (c + 1) * half)
+        got(None, wrecv.at[c], wr_r.at[c])
+        wg_ref[:, cols] = wown[:, cols] + wrecv[c].astype(F32)
     for c in range(2):
         cols = slice(c * half, (c + 1) * half)
         got(None, xrecv.at[c], xs_r.at[c])
@@ -516,37 +544,33 @@
     rows = layer_weights.shape[1]
     hbm = pl.BlockSpec(memory_space=pltpu.HBM)
     vmem = pl.BlockSpec(memory_space=pltpu.VMEM)
-    smem = pl.BlockSpec(memory_space=pltpu.SMEM)
     region = tokens // 2
     dma = pltpu.SemaphoreType.DMA
     half = width // 2
     shapes = [
-        ((tokens, width), BF),
-        ((tokens, width), BF),
         ((NZ, tokens, half), BF),
         ((2, rows, width), BF),
         ((2, NZ, tokens, half), F32),
         ((2, NZ, tokens, half), BF),
         ((2, NZ, tokens, half), BF),
         ((2, NZ, tokens, half), BF),
-        ((NZ, tokens, width), BF),
+        ((2, NZ, tokens, half), BF),
         ((width // HEAD, tokens, tokens), F32),
         ((tokens, half), BF),
         ((tokens, width), BF),
-        ((2, region, half), BF),
         ((2, NZ, region, half), BF),
         ((2, region, half), BF),
         ((2, region, half), BF),
         ((8, 1, tokens), jnp.int32),
         ((8, SPINS, width), F32),
-        ((rows, width), BF),
-        ((rows, width), BF),
+        ((2, rows, half), BF),
+        ((2, rows, half), BF),
         ((rows, width), F32),
     ]
     sems = [
-        dma((3,)), dma((2,)), dma((NZ,)), dma((NZ,)), dma((NZ,)), dma((2,)), dma((2,)),
-        dma((8,)), dma((8,)), dma((2, 3)), dma((2, 3)), dma((2, 2, NZ)), dma((2, 2, NZ)),
-        dma((2, NZ)), dma((2, NZ)), dma((2,)), dma((2,)), dma((8,)), dma((8,)), dma, dma,
+        dma((7,)), dma((2,)), dma((NZ,)), dma((NZ,)), dma((NZ,)), dma((2,)), dma((2,)),
+        dma((8,)), dma((8,)), dma((2, 2, 3)), dma((2, 2, 3)), dma((2, 2, NZ)), dma((2, 2, NZ)),
+        dma((2, 2, 3)), dma((2, 2, 3)), dma((2,)), dma((2,)), dma((8,)), dma((8,)), dma((2,)), dma((2,)),
     ]
     wg, cot, emb = pl.pallas_call(
         kernel,
@@ -555,11 +579,20 @@
             jax.ShapeDtypeStruct((tokens, width), BF),
             jax.ShapeDtypeStruct((SPINS, width), F32),
         ],
-        in_specs=[hbm, hbm, hbm, smem, vmem, smem, vmem],
+        in_specs=[hbm] * 7,
         out_specs=[vmem] * 3,
-        scratch_shapes=[pltpu.VMEM(a, b) for a, b in shapes] + sems,
+        scratch_shapes=[
+            pltpu.VMEM((tokens, width), BF),
+            pltpu.VMEM((tokens, width), BF),
+            pltpu.SMEM((2, 2), jnp.int32),
+            pltpu.VMEM((1, tokens), jnp.int32),
+            pltpu.SMEM((8,), jnp.int32),
+            pltpu.VMEM((1, tokens), jnp.int32),
+        ]
+        + [pltpu.VMEM(a, b) for a, b in shapes]
+        + sems,
         compiler_params=pltpu.CompilerParams(
-            collective_id=0, has_side_effects=True, vmem_limit_bytes=48 * 1024 * 1024
+            collective_id=0, has_side_effects=True, vmem_limit_bytes=64 * 1024 * 1024 - 65536 - 1400 * 1024
         ),
     )(
         stored_inputs[0, 0], top_cotangent[0], layer_weights[0], block_layout[0],

time: 60.6 us -> 61.2 us (level)
  Pallas kernels: 53.8 us -> 56.7 us
  local copies, waits for them, and re-layouts: 5.89 us -> 3.66 us
    pallas_call x1, Pallas kernels: 53.8 us -> 56.7 us  [one_layer(): pl.pallas_call(kernel, out_shape=[jax.ShapeDtypeStruct((rows, width), F32...]
    unnamed x17 -> x7, local copies, waits for them, and re-layouts: 5.89 us -> 3.66 us
where the time goes in v3:
time: 61.2 us; the launch traced here: 61 us
  Pallas kernels  56.7 us (93%)
  local copies, waits for them, and re-layouts  3.66 us (6%)
  between operations  0.65 us (1%)
    pallas_call x1, Pallas kernels, one_layer(): pl.pallas_call(kernel, out_shape=[jax.ShapeDtypeStruct((rows, width), F32...  56.7 us
    unnamed x7, local copies, waits for them, and re-layouts  3.66 us

profile of v3, /device:TPU:0, one launch (start us, length us, event | category | flops | bytes accessed | tf_op | source)
XLA Modules:
  0.0 61.0 jit_solution(15166724453503215961)
XLA Ops:
  0.6 56.7 %shard_map.94 = (f32[256,1024]{1,0:T(8,128)}, bf16[128,1024]{1,0:T(8,128)(2,1)}, f32[2,1024]{1,0:T(2,128)}) custom-call(bf16[128,1024]{1,0:T(8,128)(2,1)} %bitcast.10, bf16[128,1024]{1,0:T(8,128)(2,1)} %bitcast.11, bf16[256,1024]{1,0:T(8,128)(2,1)} %bitcast.8, s32[2,2]{1,0:T(2,128)} %bitcast.12, s32[1,128]{1,0:T(1,128)} %bitcast.13, s32[8]{0:T(128)} %partner_hbm.1, ...), custom_call_target="tpu_custom_call" | custom-call | tf_op jit(solution)/shard_map/pallas_call | solution.py:575
  57.4 0.0 copy-start
  57.4 2.3 %copy.13 = f32[1,256,1024]{2,1,0:T(8,128)} copy(f32[1,256,1024]{2,1,0:T(8,128)} %bitcast.7) | data formatting | bytes 2097152
  59.7 0.0 copy-done
  59.7 0.0 copy-start.1
  59.7 0.7 %copy.14 = bf16[1,1,128,1024]{3,2,1,0:T(8,128)(2,1)} copy(bf16[1,1,128,1024]{3,2,1,0:T(8,128)(2,1)S(1)} %bitcast.9) | data formatting | bytes 524288
  60.4 0.0 copy-done.1
  60.4 0.6 copy.15
Async XLA Ops:
  57.4 2.4 %copy-start = (bf16[128,1024]{1,0:T(8,128)(2,1)S(1)}, bf16[128,1024]{1,0:T(8,128)(2,1)}, u32[]{:S(2)}) copy-start(bf16[128,1024]{1,0:T(8,128)(2,1)} %get-tuple-element.7) | copy-start | bytes 786436
  59.7 0.7 %copy-start.1 = (f32[2,1024]{1,0:T(2,128)S(1)}, f32[2,1024]{1,0:T(2,128)}, u32[]{:S(2)}) copy-start(f32[2,1024]{1,0:T(2,128)} %get-tuple-element.14) | copy-start | bytes 24580

commit v4 on v3

--- a/solution.py
+++ b/solution.py
@@ -535,6 +535,18 @@
             make().wait_send()
         else:
             pl.when(cond)(lambda make=make: make().wait_send())
+
+
+def put_out(wg_ref, cot_ref, emb_ref, wg_out, cot_out, emb_out, done):
+    copies = [
+        pltpu.make_async_copy(wg_ref, wg_out, done.at[0]),
+        pltpu.make_async_copy(cot_ref, cot_out, done.at[1]),
+        pltpu.make_async_copy(emb_ref, emb_out, done.at[2]),
+    ]
+    for copy in copies:
+        copy.start()
+    for copy in copies:
+        copy.wait()
 
 
 def one_layer(
@@ -592,12 +604,26 @@
         + [pltpu.VMEM(a, b) for a, b in shapes]
         + sems,
         compiler_params=pltpu.CompilerParams(
-            collective_id=0, has_side_effects=True, vmem_limit_bytes=64 * 1024 * 1024 - 65536 - 1400 * 1024
+            collective_id=0, has_side_effects=True, vmem_limit_bytes=48 * 1024 * 1024
         ),
     )(
-        stored_inputs[0, 0], top_cotangent[0], layer_weights[0], block_layout[0],
-        region_mask[None], partner_samples, spins,
-    )
+        *[
+            pltpu.with_memory_space_constraint(value, pltpu.HBM)
+            for value in (
+                stored_inputs[0, 0], top_cotangent[0], layer_weights[0], block_layout[0],
+                region_mask[None], partner_samples, spins,
+            )
+        ]
+    )
+    anywhere = pl.BlockSpec(memory_space=pl.ANY)
+    wg, cot, emb = pl.pallas_call(
+        put_out,
+        out_shape=[jax.ShapeDtypeStruct(a.shape, a.dtype) for a in (wg, cot, emb)],
+        in_specs=[vmem] * 3,
+        out_specs=[anywhere] * 3,
+        scratch_shapes=[dma((3,))],
+        compiler_params=pltpu.CompilerParams(vmem_limit_bytes=8 * 1024 * 1024),
+    )(wg, cot, emb)
     return wg[None], cot[None, None], emb
 
 

time: 61.2 us -> 57.5 us (0.940)
  local copies, waits for them, and re-layouts: 3.66 us -> 0 us
    unnamed x7 -> x0, local copies, waits for them, and re-layouts: 3.66 us -> none
    pallas_call x0 -> x1, Pallas kernels: none -> 1.08 us  [one_layer(): pl.pallas_call(put_out, out_shape=[jax.ShapeDtypeStruct(a.shape, a.dtype)...]
    pallas_call x1, Pallas kernels: 56.7 us -> 55.6 us  [one_layer(): pl.pallas_call(kernel, out_shape=[jax.ShapeDtypeStruct((rows, width), F32...]
where the time goes in v4:
time: 57.5 us; the launch traced here: 57.4 us
  Pallas kernels  56.7 us (99%)
  between operations  0.64 us (1%)
    pallas_call x1, Pallas kernels, one_layer(): pl.pallas_call(kernel, out_shape=[jax.ShapeDtypeStruct((rows, width), F32...  55.6 us

profile of v4, /device:TPU:0, one launch (start us, length us, event | category | flops | bytes accessed | tf_op | source)
XLA Modules:
  0.0 57.4 jit_solution(425832522639987538)
XLA Ops:
  0.6 55.6 %shard_map.94 = (f32[256,1024]{1,0:T(8,128)S(1)}, bf16[128,1024]{1,0:T(8,128)(2,1)S(1)}, f32[2,1024]{1,0:T(2,128)S(1)}) custom-call(bf16[128,1024]{1,0:T(8,128)(2,1)} %bitcast.8, bf16[128,1024]{1,0:T(8,128)(2,1)} %bitcast.9, bf16[256,1024]{1,0:T(8,128)(2,1)} %bitcast.7, s32[2,2]{1,0:T(2,128)} %bitcast.10, s32[1,128]{1,0:T(1,128)} %bitcast.11, s32[8]{0:T(128)} %partner_hbm.1, ...), custom_call_target="tpu_custom_call" | custom-call | tf_op jit(solution)/shard_map/pallas_call | solution.py:587
  56.3 1.1 %shard_map.95 = (f32[256,1024]{1,0:T(8,128)}, bf16[128,1024]{1,0:T(8,128)(2,1)}, f32[2,1024]{1,0:T(2,128)}) custom-call(f32[256,1024]{1,0:T(8,128)S(1)} %get-tuple-element.9.wg_ref, bf16[128,1024]{1,0:T(8,128)(2,1)S(1)} %get-tuple-element.10.cot_ref, f32[2,1024]{1,0:T(2,128)S(1)} %get-tuple-element.11.emb_ref), custom_call_target="tpu_custom_call" | custom-call | tf_op jit(solution)/shard_map/pallas_call | solution.py:619
